TPU v7x, 128 devices: a whole 4x4x4 slice. The times are simulated.
128 devices in a mesh: dp: 32 (over y, z, core), expert: 4 (over x).
Axes of the slice: x: 4, y: 4, z: 4, core: 2. Of those that a mesh axis runs over, the one named last changes fastest.
Arguments:
- grad_parts: bfloat16 [32, 2048, 6144], P('dp', 'expert')
- bucket_order: int32 [256], replicated, may hold values from 0 to 255, each once
- master: float32 [4, 32, 16, 6144], P('expert', 'dp'), may hold values from -6 to 6
- first_moment: float32 [4, 32, 16, 6144], P('expert', 'dp'), may hold values from -0.6 to 0.6
- second_moment: float32 [4, 32, 16, 6144], P('expert', 'dp'), may hold values from 0.01 to 1
- step_count: int32 [4, 32, 16], P('expert', 'dp'), may hold values from 1 to 8
- max_rms: float32 [1], replicated, may hold values from 0.3 to 1
Outputs:
- new_master: float32 [4, 32, 16, 6144], P('expert', 'dp')
- new_first: float32 [4, 32, 16, 6144], P('expert', 'dp')
- new_second: float32 [4, 32, 16, 6144], P('expert', 'dp')
- new_params: bfloat16 [2048, 6144], P('expert')
Inputs may be any that keep to these rules, and one draw needn't show every extreme that they name: bucket_order is a permutation of the 256 buckets.
All inputs are finite; a program needn't handle non-finite values.
Results may differ from a plain program's by a relative error of at most 0.0085.
Values may be sent and summed in bfloat16 or wider, within the bound.
A program may use at most 128 MiB of HBM per device.

v0:
```python
import jax
import jax.numpy as jnp
from jax import lax
from jax.sharding import Mesh
from jax.sharding import PartitionSpec as P

DP = ("dp_0", "dp_1", "dp_2")
DP_EXPERT = ("dp_0", "dp_1", "dp_2", "expert")


def by_axis(shard, axes):
    for axis in axes:
        shard = lax.psum(shard, axis)
    return shard


def shards(grad_parts, bucket_order, master, first_moment, second_moment, step_count, max_rms):
    dp_count = lax.axis_size(DP)
    local_grad = grad_parts[0]
    rows_dev, row_width = local_grad.shape
    bucket_count = bucket_order.shape[0]
    bucket_rows = rows_dev // bucket_count
    owner_rows = rows_dev // dp_count
    buckets = local_grad.reshape(bucket_count, bucket_rows, row_width)
    slotted = jnp.take(buckets, bucket_order, axis=0)
    pieces = slotted.reshape(dp_count, owner_rows, row_width)
    received = lax.all_to_all(pieces, DP, split_axis=0, concat_axis=0, tiled=True)
    owned_sum = jnp.sum(received.astype(jnp.float32), axis=0)
    square_sum = by_axis(jnp.sum(owned_sum * owned_sum), DP_EXPERT)
    entries = float(rows_dev * row_width * lax.axis_size("expert"))
    clip_factor = jnp.minimum(1.0, max_rms[0] / jnp.sqrt(square_sum / entries + 1e-06))
    clipped = clip_factor * owned_sum
    new_first = 0.9 * first_moment[0, 0] + 0.1 * clipped
    new_second = 0.95 * second_moment[0, 0] + 0.05 * clipped * clipped
    step_float = step_count[0, 0].astype(jnp.float32)[:, None]
    first_fix = 1.0 - jnp.power(jnp.float32(0.9), step_float)
    second_fix = 1.0 - jnp.power(jnp.float32(0.95), step_float)
    ratio = new_first / first_fix / (jnp.sqrt(new_second / second_fix) + 1e-08)
    old_master = master[0, 0]
    new_master = old_master - 0.1 * (ratio + 0.1 * old_master)
    fresh = new_master.astype(jnp.bfloat16)
    gathered = lax.all_gather(fresh, DP, axis=0, tiled=True)
    slot_rows = gathered.reshape(bucket_count, bucket_rows, row_width)
    placed = jnp.zeros_like(slot_rows).at[bucket_order].set(slot_rows)
    return (
        new_master[None, None],
        new_first[None, None],
        new_second[None, None],
        placed.reshape(rows_dev, row_width),
    )


def solution(mesh):
    finer = Mesh(
        mesh.devices.reshape(4, 4, 2, mesh.shape["expert"]), ("dp_0", "dp_1", "dp_2", "expert")
    )
    return jax.shard_map(
        shards,
        mesh=finer,
        in_specs=(
            P(DP, "expert", None),
            P(),
            P("expert", DP, None, None),
            P("expert", DP, None, None),
            P("expert", DP, None, None),
            P("expert", DP, None),
            P(),
        ),
        out_specs=(
            P("expert", DP, None, None),
            P("expert", DP, None, None),
            P("expert", DP, None, None),
            P("expert", None),
        ),
        check_vma=False,
    )
```

profile of v0, /device:TPU:1, one launch (start us, length us, event | category | flops | bytes accessed | tf_op | source)
XLA Modules:
  0.0 324.7 jit_solution(6990627226799949666)
XLA Ops:
  7.2 0.0 all-gather.2.cloned.1.call-start
  7.2 0.7 compare_and_fusion
  7.9 0.7 compare_select_fusion
  8.6 0.1 broadcast_in_dim.26
  8.7 0.1 copy.11
  8.8 0.1 copy.12
  8.9 12.8 %reshape_squeeze.3 = bf16[256,2,6144]{2,1,0:T(2,128)(2,1)} reshape(bf16[1,512,6144]{2,1,0:T(8,128)(2,1)} %param.7) | data formatting | bytes 12582912 | tf_op jit(solution)/shard_map/reshape;squeeze | solution.py:24
  21.7 21.4 %gather_fusion = bf16[256,2,6144]{2,1,0:T(2,128)(2,1)} fusion(bf16[256,2,6144]{2,1,0:T(2,128)(2,1)} %reshape_squeeze.3, s32[1024]{0:T(1024)S(1)} %pad_clamp_fusion), kind=kCustom, calls=%fused_computation | custom fusion | bytes 12583936 | tf_op jit(solution)/shard_map/jit(_take)/gather | solution.py:25
  43.1 13.3 %gather.7 = bf16[32,16,6144]{2,1,0:T(8,128)(2,1)} reshape(bf16[256,2,6144]{2,1,0:T(2,128)(2,1)} %gather_fusion) | data formatting | bytes 12582912 | tf_op jit(solution)/shard_map/jit(_take)/gather | solution.py:25
  56.4 3.4 %broadcast_select_fusion = bf16[32,16,6144]{2,1,0:T(8,128)(2,1)S(1)} fusion(bf16[32,16,6144]{2,1,0:T(8,128)(2,1)} %gather.7, pred[32,16]{1,0:T(8,128)(4,1)S(1)} %copy.12), kind=kLoop, calls=%fused_computation.3 | loop fusion | flops 3145728 | bytes 12583424 | tf_op jit(solution)/shard_map/jit(_take)/select_n | solution.py:25
  59.9 82.5 %all_to_all.5 = bf16[32,16,6144]{2,1,0:T(8,128)(2,1)S(1)} all-to-all(bf16[32,16,6144]{2,1,0:T(8,128)(2,1)S(1)} %broadcast_select_fusion), channel_id=1, replica_groups=mesh['dp_0'=4,'dp_1'=4,'dp_2'=2,'expert'=4] {'dp_0','dp_1','dp_2'}, dimensions={0} | all-to-all | bytes 12582912 | tf_op jit(solution)/shard_map/all_to_all | solution.py:27
  142.4 0.0 copy-start.3
  142.4 0.0 copy-start
  142.4 0.0 copy-start.1
  142.4 0.0 copy-start.2
  142.4 1.0 convert_reduce_fusion
  143.4 0.7 multiply_reduce_fusion
  144.1 7.3 %psum.28 = f32[]{:T(128)} all-reduce(f32[]{:T(128)} %multiply_reduce_fusion), channel_id=1, replica_groups=mesh['dp_0'=4,'dp_1'=4,'dp_2'=2,'expert'=4] {'dp_0'}, use_global_device_ids=true, to_apply=%region_2.3 | all-reduce | flops 1 | bytes 8 | tf_op jit(solution)/shard_map/psum | solution.py:13
  151.5 8.0 %psum.29 = f32[]{:T(128)} all-reduce(f32[]{:T(128)} %psum.28), channel_id=1, replica_groups=mesh['dp_0'=4,'dp_1'=4,'dp_2'=2,'expert'=4] {'dp_1'}, use_global_device_ids=true, to_apply=%region_3.4 | all-reduce | flops 1 | bytes 8 | tf_op jit(solution)/shard_map/psum | solution.py:13
  159.4 0.0 copy-done.3
  159.4 7.0 %psum.30 = f32[]{:T(128)} all-reduce(f32[]{:T(128)} %psum.29), channel_id=1, replica_groups=mesh['dp_0'=4,'dp_1'=4,'dp_2'=2,'expert'=4] {'dp_2'}, use_global_device_ids=true, to_apply=%region_4.5 | all-reduce | flops 1 | bytes 8 | tf_op jit(solution)/shard_map/psum | solution.py:13
  167.0 9.3 %psum.31 = f32[]{:T(128)} all-reduce(f32[]{:T(128)} %psum.30), channel_id=1, replica_groups=mesh['dp_0'=4,'dp_1'=4,'dp_2'=2,'expert'=4] {'expert'}, use_global_device_ids=true, to_apply=%region_5.6 | all-reduce | flops 1 | bytes 8 | tf_op jit(solution)/shard_map/psum | solution.py:13
  177.0 0.0 copy-done
  177.0 0.0 copy-done.1
  177.0 0.0 copy-done.2
  177.1 1.0 fusion.9
  178.1 0.0 all-gather.2.cloned.1.call-update
  178.1 1.2 multiply_subtract_fusion
  179.3 45.1 %all-gather.2.cloned.1.call-done = bf16[512,6144]{1,0:T(8,128)(2,1)} async-done(((bf16[16,6144]{1,0:T(8,128)(2,1)}), bf16[512,6144]{1,0:T(8,128)(2,1)}) %all-gather.2.cloned.1.call-update) | async-done | bytes 6291472 | tf_op jit(solution)/shard_map/all_gather | solution.py:42
  224.4 12.8 %reshape.105 = bf16[256,2,6144]{2,1,0:T(2,128)(2,1)} reshape(bf16[512,6144]{1,0:T(8,128)(2,1)} %all-gather.2.cloned.1.call-done) | data formatting | bytes 12582912 | tf_op jit(solution)/shard_map/reshape | solution.py:43
  237.2 5.9 %broadcast_in_dim.32 = bf16[256,2,6144]{2,1,0:T(2,128)(2,1)} broadcast(bf16[]{:T(256)} %constant.13.clone.1), dimensions={} | broadcast | bytes 6291458 | tf_op jit(solution)/shard_map/broadcast_in_dim | solution.py:44
  243.1 61.5 %scatter_fusion = bf16[256,2,6144]{2,1,0:T(2,128)(2,1)} fusion(bf16[256,2,6144]{2,1,0:T(2,128)(2,1)} %broadcast_in_dim.32, s32[256]{0:T(256)S(1)} %compare_select_fusion, bf16[256,2,6144]{2,1,0:T(2,128)(2,1)} %reshape.105), kind=kCustom, calls=%fused_computation.1 | custom fusion | bytes 18875392 | tf_op jit(solution)/shard_map/scatter | solution.py:44
  304.6 13.3 %reshape.92 = bf16[512,6144]{1,0:T(8,128)(2,1)} reshape(bf16[256,2,6144]{2,1,0:T(2,128)(2,1)} %scatter_fusion) | data formatting | bytes 12582912 | tf_op jit(solution)/shard_map/reshape | solution.py:49
  (4 shorter events, 0.0 us)
Async XLA Ops:
  7.2 217.2 %all-gather.2.cloned.1.call-start = ((), (), s32[]{:S(2)}) async-start(), calls=%async_computation.1 | async-start | bytes 6488064 | tf_op jit(solution)/shard_map/all_gather | solution.py:42
  142.4 17.0 %copy-start.3 = (s32[1,1,16]{2,1,0:T(1,128)S(1)}, s32[1,1,16]{2,1,0:T(1,128)}, u32[]{:S(2)}) copy-start(s32[1,1,16]{2,1,0:T(1,128)} %param.12) | copy-start | bytes 196
  142.4 34.6 %copy-start = (f32[1,1,16,6144]{3,2,1,0:T(8,128)S(1)}, f32[1,1,16,6144]{3,2,1,0:T(8,128)}, u32[]{:S(2)}) copy-start(f32[1,1,16,6144]{3,2,1,0:T(8,128)} %param.9) | copy-start | bytes 1179652
  142.4 34.7 %copy-start.1 = (f32[1,1,16,6144]{3,2,1,0:T(8,128)S(1)}, f32[1,1,16,6144]{3,2,1,0:T(8,128)}, u32[]{:S(2)}) copy-start(f32[1,1,16,6144]{3,2,1,0:T(8,128)} %param.11) | copy-start | bytes 1179652
  142.4 34.7 %copy-start.2 = (f32[1,1,16,6144]{3,2,1,0:T(8,128)S(1)}, f32[1,1,16,6144]{3,2,1,0:T(8,128)}, u32[]{:S(2)}) copy-start(f32[1,1,16,6144]{3,2,1,0:T(8,128)} %param.10) | copy-start | bytes 1179652
Sparse Core Ops, SparseCore 0:
  178.2 46.1 all-gather.1
where the time goes:
time: 327 us; the launch traced here: 325 us
  local copies, waits for them, and re-layouts  141 us (43%)
  blocking collectives  114 us (35%)
  waiting for transfers between devices  45.1 us (14%)
  between operations  15.4 us (5%)
  other arithmetic  8.79 us (3%)
    all_to_all x1, blocking collectives, shards(): lax.all_to_all(pieces, DP, split_axis=0, concat_axis=0, tiled=True)  82.5 us
    scatter x1, local copies, waits for them, and re-layouts, shards(): placed = jnp.zeros_like(slot_rows).at[bucket_order].set(slot_rows)  61.5 us
    all_gather x1, waiting for transfers between devices, shards(): gathered = lax.all_gather(fresh, DP, axis=0, tiled=True)  45.1 us
    gather x2, local copies, waits for them, and re-layouts, shards(): slotted = jnp.take(buckets, bucket_order, axis=0)  34.7 us
    psum x4, blocking collectives, by_axis(): shard = lax.psum(shard, axis)  31.5 us
    reshape x1, local copies, waits for them, and re-layouts, shards(): placed.reshape(rows_dev, row_width)  13.3 us
    another operation x1, local copies, waits for them, and re-layouts, shards(): buckets = local_grad.reshape(bucket_count, bucket_rows, row_width)  12.8 us
    reshape x1, local copies, waits for them, and re-layouts, shards(): slot_rows = gathered.reshape(bucket_count, bucket_rows, row_width)  12.8 us
  transfers between devices with their start and end apart: 1, of which 1 were waited for; matrix products, arithmetic and copies ran while one was open for 0% of the time, Pallas kernels for 0%

commit v1 on v0

--- a/solution.py
+++ b/solution.py
@@ -10,7 +10,7 @@
 
 def by_axis(shard, axes):
     for axis in axes:
-        shard = lax.psum(shard, axis)
+        shard = jnp.sum(lax.all_gather(shard, axis), axis=0)
     return shard
 
 

time: 327 us -> 355 us (1.086)
  waiting for transfers between devices: 45.1 us -> 123 us
  blocking collectives: 114 us -> 37.8 us
  starting transfers between devices: 0.04 us -> 9.82 us
  local copies, waits for them, and re-layouts: 141 us -> 149 us
  other arithmetic: 8.79 us -> 16.7 us
    all_to_all x1 -> x0, blocking collectives: 82.5 us -> none  [shards(): lax.all_to_all(pieces, DP, split_axis=0, concat_axis=0, tiled=True)]
    all_to_all x0 -> x1, waiting for transfers between devices: none -> 77.2 us  [shards(): lax.all_to_all(pieces, DP, split_axis=0, concat_axis=0, tiled=True)]
    unnamed x0 -> x4, blocking collectives: none -> 37.8 us
    psum x4 -> x0, blocking collectives: 31.5 us -> none  [by_axis(): shard = lax.psum(shard, axis)]
    all_to_all x0 -> x1, starting transfers between devices: none -> 9.78 us  [shards(): lax.all_to_all(pieces, DP, split_axis=0, concat_axis=0, tiled=True)]
    unnamed x8 -> x28, local copies, waits for them, and re-layouts: 0.01 us -> 7.99 us
  transfers between devices with their start and end apart: 1 -> 2, of which waited for: 1 -> 2; matrix products, arithmetic and copies ran while one was open for 0% -> 1% of each run, Pallas kernels for 0% -> 0%
where the time goes in v1:
time: 355 us; the launch traced here: 353 us
  local copies, waits for them, and re-layouts  149 us (42%)
  waiting for transfers between devices  123 us (35%)
  blocking collectives  37.8 us (11%)
  other arithmetic  16.7 us (5%)
  between operations  15.5 us (4%)
  starting transfers between devices  9.82 us (3%)
    all_to_all x1, waiting for transfers between devices, shards(): lax.all_to_all(pieces, DP, split_axis=0, concat_axis=0, tiled=True)  77.2 us
    scatter x1, local copies, waits for them, and re-layouts, shards(): placed = jnp.zeros_like(slot_rows).at[bucket_order].set(slot_rows)  61.5 us
    all_gather x1, waiting for transfers between devices, shards(): gathered = lax.all_gather(fresh, DP, axis=0, tiled=True)  46.2 us
    unnamed x4, blocking collectives  37.8 us
    gather x2, local copies, waits for them, and re-layouts, shards(): slotted = jnp.take(buckets, bucket_order, axis=0)  34.7 us
    reshape x1, local copies, waits for them, and re-layouts, shards(): placed.reshape(rows_dev, row_width)  13.3 us
    another operation x1, local copies, waits for them, and re-layouts, shards(): buckets = local_grad.reshape(bucket_count, bucket_rows, row_width)  12.8 us
    reshape x1, local copies, waits for them, and re-layouts, shards(): slot_rows = gathered.reshape(bucket_count, bucket_rows, row_width)  12.8 us
  transfers between devices with their start and end apart: 2, of which 2 were waited for; matrix products, arithmetic and copies ran while one was open for 1% of the time, Pallas kernels for 0%

profile of v1, /device:TPU:1, one launch (start us, length us, event | category | flops | bytes accessed | tf_op | source)
XLA Modules:
  0.0 352.7 jit_solution(7678218674586095203)
XLA Ops:
  7.2 0.7 compare_and_fusion
  7.9 0.7 compare_select_fusion
  8.5 0.1 broadcast_in_dim.26
  8.6 0.1 copy.11
  8.7 0.1 copy.12
  8.9 12.8 %reshape_squeeze.3 = bf16[256,2,6144]{2,1,0:T(2,128)(2,1)} reshape(bf16[1,512,6144]{2,1,0:T(8,128)(2,1)} %param.7) | data formatting | bytes 12582912 | tf_op jit(solution)/shard_map/reshape;squeeze | solution.py:24
  21.7 21.4 %gather_fusion = bf16[256,2,6144]{2,1,0:T(2,128)(2,1)} fusion(bf16[256,2,6144]{2,1,0:T(2,128)(2,1)} %reshape_squeeze.3, s32[1024]{0:T(1024)S(1)} %pad_clamp_fusion), kind=kCustom, calls=%fused_computation | custom fusion | bytes 12583936 | tf_op jit(solution)/shard_map/jit(_take)/gather | solution.py:25
  43.1 13.3 %gather.7 = bf16[32,16,6144]{2,1,0:T(8,128)(2,1)} reshape(bf16[256,2,6144]{2,1,0:T(2,128)(2,1)} %gather_fusion) | data formatting | bytes 12582912 | tf_op jit(solution)/shard_map/jit(_take)/gather | solution.py:25
  56.4 6.2 %broadcast_select_fusion = bf16[32,16,6144]{2,1,0:T(8,128)(2,1)} fusion(bf16[32,16,6144]{2,1,0:T(8,128)(2,1)} %gather.7, pred[32,16]{1,0:T(8,128)(4,1)S(1)} %copy.12), kind=kLoop, calls=%fused_computation.3 | loop fusion | flops 3145728 | bytes 12583424 | tf_op jit(solution)/shard_map/jit(_take)/select_n | solution.py:25
  62.5 0.0 copy-start.7
  62.5 0.0 copy-start.3
  62.5 9.8 %all-to-all-start = ((bf16[32,16,6144]{2,1,0:T(8,128)(2,1)}), bf16[32,16,6144]{2,1,0:T(8,128)(2,1)}, u32[]{:S(2)}, u32[]{:S(2)}) async-start(bf16[32,16,6144]{2,1,0:T(8,128)(2,1)} %broadcast_select_fusion), calls=%async_computation | async-start | bytes 12582912 | tf_op jit(solution)/shard_map/all_to_all | solution.py:27
  72.3 0.0 copy-start.6
  72.3 0.0 copy-start.5
  72.4 0.0 copy-start.4
  72.4 0.0 copy-start
  72.4 0.0 copy-start.1
  72.4 0.0 copy-start.2
  72.4 0.0 all-gather.2.cloned.1.call-start
  72.5 0.0 copy-done.7
  72.5 0.6 dynamic-slice
  73.1 0.0 copy-done.3
  73.1 77.2 %all-to-all-done = bf16[32,16,6144]{2,1,0:T(8,128)(2,1)} async-done(((bf16[32,16,6144]{2,1,0:T(8,128)(2,1)}), bf16[32,16,6144]{2,1,0:T(8,128)(2,1)}, u32[]{:S(2)}, u32[]{:S(2)}) %all-to-all-start) | async-done | bytes 6291488 | tf_op jit(solution)/shard_map/all_to_all | solution.py:27
  150.3 3.8 %convert_reduce_fusion = f32[16,6144]{1,0:T(8,128)S(1)} fusion(bf16[32,16,6144]{2,1,0:T(8,128)(2,1)} %all-to-all-done), kind=kLoop, calls=%fused_computation.2 | loop fusion | flops 6193152 | bytes 6684672 | tf_op jit(solution)/shard_map/reduce_sum | solution.py:28
  154.1 0.7 multiply_reduce_fusion
  154.8 1.4 dynamic-update-slice
  156.2 0.0 copy-done.6
  156.2 0.6 dynamic-slice.1
  156.8 7.7 %all-reduce = f32[4]{0:T(128)S(1)} all-reduce(f32[4]{0:T(128)S(1)} %dynamic-update-slice), channel_id=1, replica_groups=mesh['dp_0'=4,'dp_1'=4,'dp_2'=2,'expert'=4] {'dp_0'}, use_global_device_ids=true, to_apply=%add | all-reduce | flops 4 | bytes 32
  164.5 0.6 reduce_sum.56
  165.1 1.4 dynamic-update-slice.1
  166.5 0.0 copy-done.5
  166.5 0.6 dynamic-slice.2
  167.1 14.7 %all-reduce.1 = f32[4]{0:T(128)S(1)} all-reduce(f32[4]{0:T(128)S(1)} %dynamic-update-slice.1), channel_id=1, replica_groups=mesh['dp_0'=4,'dp_1'=4,'dp_2'=2,'expert'=4] {'dp_1'}, use_global_device_ids=true, to_apply=%add.1 | all-reduce | flops 4 | bytes 32
  181.8 0.6 reduce_sum.57
  182.5 1.4 dynamic-update-slice.2
  183.9 0.0 copy-done.4
  183.9 0.6 dynamic-slice.3
  184.4 6.7 %all-reduce.2 = f32[2]{0:T(128)S(1)} all-reduce(f32[2]{0:T(128)S(1)} %dynamic-update-slice.2), channel_id=1, replica_groups=mesh['dp_0'=4,'dp_1'=4,'dp_2'=2,'expert'=4] {'dp_2'}, use_global_device_ids=true, to_apply=%add.2 | all-reduce | flops 2 | bytes 16
  191.2 0.6 reduce_sum.58
  191.8 1.4 dynamic-update-slice.3
  193.8 8.7 %all-reduce.3 = f32[4]{0:T(128)S(1)} all-reduce(f32[4]{0:T(128)S(1)} %dynamic-update-slice.3), channel_id=1, replica_groups=mesh['dp_0'=4,'dp_1'=4,'dp_2'=2,'expert'=4] {'expert'}, use_global_device_ids=true, to_apply=%add.3 | all-reduce | flops 4 | bytes 32
  202.5 0.6 reduce_sum.59
  203.8 0.0 copy-done
  203.8 0.0 copy-done.1
  203.8 0.0 copy-done.2
  203.8 1.0 fusion.9
  204.9 0.0 all-gather.2.cloned.1.call-update
  204.9 1.2 multiply_subtract_fusion
  206.1 46.2 %all-gather.2.cloned.1.call-done = bf16[512,6144]{1,0:T(8,128)(2,1)} async-done(((bf16[16,6144]{1,0:T(8,128)(2,1)}), bf16[512,6144]{1,0:T(8,128)(2,1)}) %all-gather.2.cloned.1.call-update) | async-done | bytes 6291472 | tf_op jit(solution)/shard_map/all_gather | solution.py:42
  252.3 12.8 %reshape.105 = bf16[256,2,6144]{2,1,0:T(2,128)(2,1)} reshape(bf16[512,6144]{1,0:T(8,128)(2,1)} %all-gather.2.cloned.1.call-done) | data formatting | bytes 12582912 | tf_op jit(solution)/shard_map/reshape | solution.py:43
  265.1 5.9 %broadcast_in_dim.32 = bf16[256,2,6144]{2,1,0:T(2,128)(2,1)} broadcast(bf16[]{:T(256)} %constant.13.clone.1), dimensions={} | broadcast | bytes 6291458 | tf_op jit(solution)/shard_map/broadcast_in_dim | solution.py:44
  271.0 61.5 %scatter_fusion = bf16[256,2,6144]{2,1,0:T(2,128)(2,1)} fusion(bf16[256,2,6144]{2,1,0:T(2,128)(2,1)} %broadcast_in_dim.32, s32[256]{0:T(256)S(1)} %compare_select_fusion, bf16[256,2,6144]{2,1,0:T(2,128)(2,1)} %reshape.105), kind=kCustom, calls=%fused_computation.1 | custom fusion | bytes 18875392 | tf_op jit(solution)/shard_map/scatter | solution.py:44
  332.5 13.3 %reshape.92 = bf16[512,6144]{1,0:T(8,128)(2,1)} reshape(bf16[256,2,6144]{2,1,0:T(2,128)(2,1)} %scatter_fusion) | data formatting | bytes 12582912 | tf_op jit(solution)/shard_map/reshape | solution.py:49
  (8 shorter events, 0.1 us)
Async XLA Ops:
  62.5 9.9 %copy-start.7 = (u32[128]{0:T(128)S(1)}, u32[128]{0:T(128)}, u32[]{:S(2)}) copy-start(u32[128]{0:T(128)} %constant.49) | copy-start | bytes 1540
  62.5 10.5 %copy-start.3 = (s32[1,1,16]{2,1,0:T(1,128)S(1)}, s32[1,1,16]{2,1,0:T(1,128)}, u32[]{:S(2)}) copy-start(s32[1,1,16]{2,1,0:T(1,128)} %param.12) | copy-start | bytes 196
  62.5 87.8 %all-to-all-start = ((bf16[32,16,6144]{2,1,0:T(8,128)(2,1)}), bf16[32,16,6144]{2,1,0:T(8,128)(2,1)}, u32[]{:S(2)}, u32[]{:S(2)}) async-start(bf16[32,16,6144]{2,1,0:T(8,128)(2,1)} %broadcast_select_fusion), calls=%async_computation | async-start | bytes 12582912 | tf_op jit(solution)/shard_map/all_to_all | solution.py:27
  72.3 83.9 %copy-start.6 = (u32[128]{0:T(128)S(1)}, u32[128]{0:T(128)}, u32[]{:S(2)}) copy-start(u32[128]{0:T(128)} %constant.54) | copy-start | bytes 1540
  72.3 94.2 %copy-start.5 = (u32[128]{0:T(128)S(1)}, u32[128]{0:T(128)}, u32[]{:S(2)}) copy-start(u32[128]{0:T(128)} %constant.59) | copy-start | bytes 1540
  72.4 111.5 %copy-start.4 = (u32[128]{0:T(128)S(1)}, u32[128]{0:T(128)}, u32[]{:S(2)}) copy-start(u32[128]{0:T(128)} %constant.64) | copy-start | bytes 1540
  72.4 131.4 %copy-start = (f32[1,1,16,6144]{3,2,1,0:T(8,128)S(1)}, f32[1,1,16,6144]{3,2,1,0:T(8,128)}, u32[]{:S(2)}) copy-start(f32[1,1,16,6144]{3,2,1,0:T(8,128)} %param.9) | copy-start | bytes 1179652
  72.4 131.4 %copy-start.1 = (f32[1,1,16,6144]{3,2,1,0:T(8,128)S(1)}, f32[1,1,16,6144]{3,2,1,0:T(8,128)}, u32[]{:S(2)}) copy-start(f32[1,1,16,6144]{3,2,1,0:T(8,128)} %param.11) | copy-start | bytes 1179652
  72.4 131.4 %copy-start.2 = (f32[1,1,16,6144]{3,2,1,0:T(8,128)S(1)}, f32[1,1,16,6144]{3,2,1,0:T(8,128)}, u32[]{:S(2)}) copy-start(f32[1,1,16,6144]{3,2,1,0:T(8,128)} %param.10) | copy-start | bytes 1179652
  72.4 179.9 %all-gather.2.cloned.1.call-start = ((), (), s32[]{:S(2)}) async-start(), calls=%async_computation.1 | async-start | bytes 6488064 | tf_op jit(solution)/shard_map/all_gather | solution.py:42
Sparse Core Ops, SparseCore 0:
  205.0 47.2 all-gather.1
